TPU v7x, 512 devices: a whole 4x8x8 slice. The times are simulated.
512 devices in a mesh: sec: 32 (over y, z_hi, core), sub: 16 (over z_lo, x).
Axes of the slice: x: 4, y: 8, z: 8 (z_hi: 2, z_lo: 4; z = z_hi * 4 + z_lo), core: 2. Of those that a mesh axis runs over, the one named last changes fastest.
Arguments:
- forcing: float32 [32, 192, 64, 128], P('sec', 'sub'), may hold values from -60 to 60
- coupling: float32 [32, 192, 64, 128], P('sec', 'sub'), may hold values from -0.6 to 0.6
- diag_pair: float32 [32, 192, 64, 128], P('sec', 'sub'), may hold values from -1 to 9
- side: float32 [32, 192, 32], P('sec', 'sub'), may hold values from -1 to -0.3
- basis: float32 [32, 1024, 768], P('sec', 'sub'), may hold values from -0.21875 to 0.21875
- coarse_inverse: float32 [32, 1024, 1024], P('sec', 'sub'), may hold values from -0.05 to 0.3
Outputs:
- solution: float32 [32, 192, 64, 128], P('sec', 'sub')
All inputs are finite; a program needn't handle non-finite values.
Results may differ from a plain program's by a relative error of at most 0.0001.
Values sent between devices are 32-bit elements; how exact they have to be, the bound alone decides.
No kernel may reach another device: no remote copies, remote signals or barrier semaphores. Data moves between devices by JAX's collectives and lax.ppermute only.
A program may use at most 64 MiB of HBM per device.

v0:
```python
import jax
import jax.numpy as jnp
from jax import lax
from jax.sharding import PartitionSpec as P

SWEEPS = 4
ITERS = 2
PRECISE = lax.Precision.HIGHEST


def extended(block, sides, width):
    for axis, dim in sides:
        count = lax.axis_size(axis)
        forward = [(i, i + 1) for i in range(count - 1)]
        backward = [(target, source) for source, target in forward]
        low = lax.ppermute(
            lax.slice_in_dim(block, block.shape[dim] - width, None, axis=dim), axis, forward
        )
        high = lax.ppermute(lax.slice_in_dim(block, 0, width, axis=dim), axis, backward)
        block = jnp.concatenate([low, block, high], axis=dim)
    return block


def from_behind(value, axis, steps):
    count = lax.axis_size(axis)
    initial, last = (max(0, -steps), min(count, count - steps))
    return lax.ppermute(value, axis, [(source, source + steps) for source in range(initial, last)])


def tile_apply(tile_set, vector):
    return jnp.einsum("bij,bjc->bic", tile_set, vector, precision=PRECISE)


def couple(coupling, diagonal, centre, before, after):
    return tile_apply(diagonal, centre) + tile_apply(
        coupling, jnp.concatenate([before, after], axis=1)
    )


def chain_apply(coupling, diagonal, vector):
    zero_block = jnp.zeros_like(vector[:1])
    before = jnp.concatenate([zero_block, vector[:-1]], axis=0)
    after = jnp.concatenate([vector[1:], zero_block], axis=0)
    return couple(coupling, diagonal, vector, before, after)


def add_faces(linear, sides, below, above):
    face_rows = sides.shape[-1] // 2
    node_count = linear.shape[1]
    lower_term = sides[:, :face_rows, None] * below
    upper_term = sides[:, face_rows:, None] * above
    return jnp.concatenate(
        [
            linear[:, :face_rows] + lower_term,
            linear[:, face_rows : node_count - face_rows],
            linear[:, node_count - face_rows :] + upper_term,
        ],
        axis=1,
    )


def local_sweeps(residual_ext, coupling_ext, diagonal_ext, inverse_ext):
    update = tile_apply(inverse_ext, residual_ext)
    for sweep_index in range(SWEEPS - 1):
        update = update + tile_apply(
            inverse_ext, residual_ext - chain_apply(coupling_ext, diagonal_ext, update)
        )
    return update[1:-1]


def project(basis_rows, field):
    return jnp.dot(basis_rows, field.reshape(-1, field.shape[-1]), precision=PRECISE)


def expand(basis_rows, correction, target_shape):
    spread = lax.dot_general(basis_rows, correction, (((0,), (0,)), ((), ())), precision=PRECISE)
    return spread.reshape(target_shape)


def fold_rows(inverse_rows, segment):
    return jnp.dot(inverse_rows, segment, precision=PRECISE)


def coarse_direct(basis_rows, inverse_rows, residual):
    projected = project(basis_rows, residual)
    return fold_rows(inverse_rows, lax.all_gather(projected, "sub", axis=0, tiled=True))


def operate(update, coupling, diagonal, sides):
    update_ext = extended(update, (("sub", 0),), 1)
    linear = couple(coupling, diagonal, update, update_ext[:-2], update_ext[2:])
    face_rows = sides.shape[-1] // 2
    node_count = update.shape[1]
    north_face = update[:, node_count - face_rows :, :]
    south_face = update[:, :face_rows, :]
    below = from_behind(north_face, "sec", 1)
    above = from_behind(south_face, "sec", -1)
    return add_faces(linear, sides, below, above)


def step_length(image, residual):
    numerator, denominator = lax.psum(
        (jnp.sum(image * residual, axis=(0, 1)), jnp.sum(image * image, axis=(0, 1))),
        ("sec", "sub"),
    )
    return numerator / denominator


def shards(forcing, coupling, diag_pair, side, basis, coarse_inverse):
    residual = forcing[0]
    couplings = coupling[0]
    pairs = diag_pair[0]
    sides = side[0]
    basis_rows = basis[0]
    inverse_rows = coarse_inverse[0]
    node_count = residual.shape[1]
    stacked = jnp.concatenate([couplings, pairs], axis=2)
    stacked_ext = extended(stacked, (("sub", 0),), 1)
    coupling_ext = stacked_ext[:, :, : 2 * node_count]
    diagonal_ext = stacked_ext[:, :, 2 * node_count : 3 * node_count]
    inverse_ext = stacked_ext[:, :, 3 * node_count :]
    diagonal_own = pairs[:, :, :node_count]
    solution = jnp.zeros_like(residual)
    for iteration in range(ITERS):
        correction = coarse_direct(basis_rows, inverse_rows, residual)
        residual_ext = extended(residual, (("sub", 0),), 1)
        local_part = local_sweeps(residual_ext, coupling_ext, diagonal_ext, inverse_ext)
        update = local_part + expand(basis_rows, correction, residual.shape)
        image = operate(update, couplings, diagonal_own, sides)
        step_size = step_length(image, residual)
        solution = solution + step_size * update
        residual = residual - step_size * image
    return solution[None]


def solution(mesh):
    placed = (
        P("sec", "sub", None, None),
        P("sec", "sub", None, None),
        P("sec", "sub", None, None),
        P("sec", "sub", None),
        P("sec", "sub", None),
        P("sec", "sub", None),
    )
    return jax.shard_map(
        shards, mesh=mesh, in_specs=placed, out_specs=P("sec", "sub", None, None), check_vma=False
    )
```

profile of v0, /device:TPU:1, one launch (start us, length us, event | category | flops | bytes accessed | tf_op | source)
XLA Modules:
  0.0 371.0 jit_solution(13853140546099342183)
XLA Ops:
  0.0 1.4 slice_bitcast_fusion.1
  1.4 3.9 %collective-permute-start.2 = (f32[1,64,128]{2,1,0:T(8,128)}, f32[1,64,128]{2,1,0:T(8,128)S(1)}, u32[]{:S(2)}, u32[]{:S(2)}) collective-permute-start(f32[1,64,128]{2,1,0:T(8,128)} %get-tuple-element.43), channel_id=1, source_target_pairs={{0,1},{1,2},{2,3},{3,4},{4,5},{5,6},{6,7},{7,8},{8,9},{9,10},{10,1... | collective-permute-start | bytes 98312 | tf_op jit(solution)/shard_map/ppermute | solution.py:16
  5.4 1.3 collective-permute-start.3
  6.7 0.9 pad_maximum_fusion.12
  7.6 4.6 %collective-permute-start = (f32[1,64,256]{2,1,0:T(8,128)S(1)}, f32[1,64,256]{2,1,0:T(8,128)}, u32[]{:S(2)}, u32[]{:S(2)}) collective-permute-start(f32[1,64,256]{2,1,0:T(8,128)S(1)} %get-tuple-element.13), channel_id=1, source_target_pairs={{0,1},{1,2},{2,3},{3,4},{4,5},{5,6},{6,7},{7,8},{8,9},{9,10},{10,1... | collective-permute-start | bytes 196616 | tf_op jit(solution)/shard_map/ppermute | solution.py:16
  12.2 1.3 collective-permute-start.1
  13.9 41.7 %all_gather.6 = f32[1024,128]{1,0:T(8,128)S(1)} all-gather(f32[64,128]{1,0:T(8,128)S(1)} %fusion.90), channel_id=1, replica_groups=mesh['sec'=32,'sub'=16] {'sub'}, dimensions={0}, use_global_device_ids=true | all-gather | bytes 557056 | tf_op jit(solution)/shard_map/all_gather | solution.py:86
  55.6 1.0 fusion.85
  57.4 0.8 copy-done.2
  58.3 0.9 pad_maximum_fusion
  59.3 0.6 fusion.81
  60.0 0.9 fusion.28
  60.9 0.6 fusion.5
  61.5 0.6 convolution_add_fusion.8
  62.2 0.9 fusion.24
  63.7 0.6 convolution_add_fusion.6
  64.5 0.9 fusion.20
  66.0 0.6 fusion.77
  67.2 1.3 collective-permute-start.4
  68.5 1.3 collective-permute-start.5
  69.8 16.4 %collective-permute-start.6 = (f32[12,16,128]{2,1,0:T(8,128)S(1)}, f32[12,16,128]{2,1,0:T(8,128)S(1)}, u32[]{:S(2)}, u32[]{:S(2)}) collective-permute-start(f32[12,16,128]{2,1,0:T(8,128)S(1)} %get-tuple-element.39), channel_id=1, source_target_pairs={{0,16},{16,32},{32,48},{48,64},{64,80},{80,96},{96,112},{112,128},... | collective-permute-start | bytes 294920 | tf_op jit(solution)/shard_map/ppermute | solution.py:27
  86.3 1.9 collective-permute-start.7
  88.2 0.7 fusion.7
  89.0 0.7 fusion.125
  89.7 6.4 %collective-permute-done.7 = f32[12,16,128]{2,1,0:T(8,128)S(1)} collective-permute-done((f32[12,16,128]{2,1,0:T(8,128)S(1)}, f32[12,16,128]{2,1,0:T(8,128)S(1)}, u32[]{:S(2)}, u32[]{:S(2)}) %collective-permute-start.7) | collective-permute-done | bytes 98336 | tf_op jit(solution)/shard_map/ppermute | solution.py:27
  96.9 97.6 %all-reduce.13 = (f32[128]{0:T(128)S(1)}, f32[128]{0:T(128)S(1)}) all-reduce(f32[128]{0:T(128)S(1)} %get-tuple-element.8, f32[128]{0:T(128)S(1)} %get-tuple-element.7), channel_id=1, replica_groups=mesh['sec'=32,'sub'=16] {'sec','sub'}, use_global_device_ids=true, to_apply=%region_1.0 | all-reduce | flops 256 | bytes 2048 | tf_op jit(solution)/shard_map/psum | solution.py:102
  194.6 1.0 multiply_subtract_fusion
  196.1 2.2 collective-permute-start.8
  198.4 1.3 collective-permute-start.9
  199.7 35.9 %all_gather.7 = f32[1024,128]{1,0:T(8,128)S(1)} all-gather(f32[64,128]{1,0:T(8,128)S(1)} %convolution_bitcast_fusion.2), channel_id=1, replica_groups=mesh['sec'=32,'sub'=16] {'sub'}, dimensions={0}, use_global_device_ids=true | all-gather | bytes 557056 | tf_op jit(solution)/shard_map/all_gather | solution.py:86
  235.5 1.0 fusion.83
  237.0 0.9 copy.10
  237.9 0.6 fusion.75
  238.7 0.9 fusion.16
  240.2 0.6 convolution_add_fusion.3
  240.9 0.9 fusion.12
  242.4 0.6 convolution_add_fusion.1
  243.2 0.9 fusion.8
  244.7 0.6 fusion.71
  246.2 1.3 collective-permute-start.10
  247.5 1.3 collective-permute-start.11
  248.9 13.5 %collective-permute-start.12 = (f32[12,16,128]{2,1,0:T(8,128)S(1)}, f32[12,16,128]{2,1,0:T(8,128)S(1)}, u32[]{:S(2)}, u32[]{:S(2)}) collective-permute-start(f32[12,16,128]{2,1,0:T(8,128)S(1)} %get-tuple-element.29), channel_id=1, source_target_pairs={{0,16},{16,32},{32,48},{48,64},{64,80},{80,96},{96,112},{112,128},... | collective-permute-start | bytes 294920 | tf_op jit(solution)/shard_map/ppermute | solution.py:27
  262.4 1.9 collective-permute-start.13
  264.3 0.7 fusion.6
  265.1 7.6 %collective-permute-done.13 = f32[12,16,128]{2,1,0:T(8,128)S(1)} collective-permute-done((f32[12,16,128]{2,1,0:T(8,128)S(1)}, f32[12,16,128]{2,1,0:T(8,128)S(1)}, u32[]{:S(2)}, u32[]{:S(2)}) %collective-permute-start.13) | collective-permute-done | bytes 98336 | tf_op jit(solution)/shard_map/ppermute | solution.py:27
  273.0 96.6 %all-reduce.12 = (f32[128]{0:T(128)S(1)}, f32[128]{0:T(128)S(1)}) all-reduce(f32[128]{0:T(128)S(1)} %get-tuple-element.6, f32[128]{0:T(128)S(1)} %get-tuple-element.5), channel_id=1, replica_groups=mesh['sec'=32,'sub'=16] {'sec','sub'}, use_global_device_ids=true, to_apply=%region_5.0 | all-reduce | flops 256 | bytes 2048 | tf_op jit(solution)/shard_map/psum | solution.py:102
  369.6 0.6 copy-done.13
  370.2 0.8 add_bitcast_fusion
  (73 shorter events, 8.2 us)
Async XLA Ops:
  0.0 55.6 %copy-start = (f32[1,64,1024]{2,1,0:T(8,128)S(1)}, f32[1,64,1024]{2,1,0:T(8,128)}, u32[]{:S(2)}) copy-start(f32[1,64,1024]{2,1,0:T(8,128)} %param.11) | copy-start | bytes 786436
  1.4 57.8 %collective-permute-start.2 = (f32[1,64,128]{2,1,0:T(8,128)}, f32[1,64,128]{2,1,0:T(8,128)S(1)}, u32[]{:S(2)}, u32[]{:S(2)}) collective-permute-start(f32[1,64,128]{2,1,0:T(8,128)} %get-tuple-element.43), channel_id=1, source_target_pairs={{0,1},{1,2},{2,3},{3,4},{4,5},{5,6},{6,7},{7,8},{8,9},{9,10},{10,1... | collective-permute-start | bytes 98312 | tf_op jit(solution)/shard_map/ppermute | solution.py:16
  5.4 53.9 %collective-permute-start.3 = (f32[1,64,128]{2,1,0:T(8,128)S(1)}, f32[1,64,128]{2,1,0:T(8,128)S(1)}, u32[]{:S(2)}, u32[]{:S(2)}) collective-permute-start(f32[1,64,128]{2,1,0:T(8,128)S(1)} %get-tuple-element.44), channel_id=1, source_target_pairs={{1,0},{2,1},{3,2},{4,3},{5,4},{6,5},{7,6},{8,7},{9,8},{10,9},{11,1... | collective-permute-start | bytes 98312 | tf_op jit(solution)/shard_map/ppermute | solution.py:19
  6.7 6.8 %copy-start.11 = (f32[1,12,32]{2,0,1:T(1,128)S(1)}, f32[1,12,32]{2,0,1:T(1,128)}, u32[]{:S(2)}) copy-start(f32[1,12,32]{2,0,1:T(1,128)} %param.9) | copy-start | bytes 4612
  6.7 6.8 %copy-start.1 = (f32[1,12,64,128]{3,2,1,0:T(8,128)S(1)}, f32[1,12,64,128]{3,2,1,0:T(8,128)}, u32[]{:S(2)}) copy-start(f32[1,12,64,128]{3,2,1,0:T(8,128)} %param.6) | copy-start | bytes 1179652
  6.7 6.8 %copy-start.4 = (f32[1,64,768]{2,1,0:T(8,128)S(1)}, f32[1,64,768]{2,1,0:T(8,128)}, u32[]{:S(2)}) copy-start(f32[1,64,768]{2,1,0:T(8,128)} %param.10) | copy-start | bytes 589828
  7.6 49.8 %collective-permute-start = (f32[1,64,256]{2,1,0:T(8,128)S(1)}, f32[1,64,256]{2,1,0:T(8,128)}, u32[]{:S(2)}, u32[]{:S(2)}) collective-permute-start(f32[1,64,256]{2,1,0:T(8,128)S(1)} %get-tuple-element.13), channel_id=1, source_target_pairs={{0,1},{1,2},{2,3},{3,4},{4,5},{5,6},{6,7},{7,8},{8,9},{9,10},{10,1... | collective-permute-start | bytes 196616 | tf_op jit(solution)/shard_map/ppermute | solution.py:16
  12.2 45.2 %collective-permute-start.1 = (f32[1,64,256]{2,1,0:T(8,128)S(1)}, f32[1,64,256]{2,1,0:T(8,128)}, u32[]{:S(2)}, u32[]{:S(2)}) collective-permute-start(f32[1,64,256]{2,1,0:T(8,128)S(1)} %get-tuple-element.14), channel_id=1, source_target_pairs={{1,0},{2,1},{3,2},{4,3},{5,4},{6,5},{7,6},{8,7},{9,8},{10,9},{11,1... | collective-permute-start | bytes 196616 | tf_op jit(solution)/shard_map/ppermute | solution.py:19
  57.2 1.0 copy-start.2
  57.2 1.1 copy-start.3
  67.2 21.0 %collective-permute-start.4 = (f32[1,64,128]{2,1,0:T(8,128)S(1)}, f32[1,64,128]{2,1,0:T(8,128)S(1)}, u32[]{:S(2)}, u32[]{:S(2)}) collective-permute-start(f32[1,64,128]{2,1,0:T(8,128)S(1)} %get-tuple-element.41), channel_id=1, source_target_pairs={{0,1},{1,2},{2,3},{3,4},{4,5},{5,6},{6,7},{7,8},{8,9},{9,10},{10,1... | collective-permute-start | bytes 98312 | tf_op jit(solution)/shard_map/ppermute | solution.py:16
  68.5 19.7 %collective-permute-start.5 = (f32[1,64,128]{2,1,0:T(8,128)S(1)}, f32[1,64,128]{2,1,0:T(8,128)S(1)}, u32[]{:S(2)}, u32[]{:S(2)}) collective-permute-start(f32[1,64,128]{2,1,0:T(8,128)S(1)} %get-tuple-element.42), channel_id=1, source_target_pairs={{1,0},{2,1},{3,2},{4,3},{5,4},{6,5},{7,6},{8,7},{9,8},{10,9},{11,1... | collective-permute-start | bytes 98312 | tf_op jit(solution)/shard_map/ppermute | solution.py:19
  69.8 19.9 %collective-permute-start.6 = (f32[12,16,128]{2,1,0:T(8,128)S(1)}, f32[12,16,128]{2,1,0:T(8,128)S(1)}, u32[]{:S(2)}, u32[]{:S(2)}) collective-permute-start(f32[12,16,128]{2,1,0:T(8,128)S(1)} %get-tuple-element.39), channel_id=1, source_target_pairs={{0,16},{16,32},{32,48},{48,64},{64,80},{80,96},{96,112},{112,128},... | collective-permute-start | bytes 294920 | tf_op jit(solution)/shard_map/ppermute | solution.py:27
  86.3 9.8 %collective-permute-start.7 = (f32[12,16,128]{2,1,0:T(8,128)S(1)}, f32[12,16,128]{2,1,0:T(8,128)S(1)}, u32[]{:S(2)}, u32[]{:S(2)}) collective-permute-start(f32[12,16,128]{2,1,0:T(8,128)S(1)} %get-tuple-element.40), channel_id=1, source_target_pairs={{16,0},{32,16},{48,32},{64,48},{80,64},{96,80},{112,96},{128,112},... | collective-permute-start | bytes 294920 | tf_op jit(solution)/shard_map/ppermute | solution.py:27
  96.2 0.6 copy-start.5
  96.2 0.7 copy-start.7
  194.6 1.1 copy-start.12
  194.6 1.1 copy-start.6
  194.6 1.1 copy-start.8
  194.6 1.1 copy-start.10
  196.1 41.8 %collective-permute-start.8 = (f32[1,64,128]{2,1,0:T(8,128)S(1)}, f32[1,64,128]{2,1,0:T(8,128)S(1)}, u32[]{:S(2)}, u32[]{:S(2)}) collective-permute-start(f32[1,64,128]{2,1,0:T(8,128)S(1)} %get-tuple-element.33), channel_id=1, source_target_pairs={{0,1},{1,2},{2,3},{3,4},{4,5},{5,6},{6,7},{7,8},{8,9},{9,10},{10,1... | collective-permute-start | bytes 98312 | tf_op jit(solution)/shard_map/ppermute | solution.py:16
  198.4 39.6 %collective-permute-start.9 = (f32[1,64,128]{2,1,0:T(8,128)S(1)}, f32[1,64,128]{2,1,0:T(8,128)S(1)}, u32[]{:S(2)}, u32[]{:S(2)}) collective-permute-start(f32[1,64,128]{2,1,0:T(8,128)S(1)} %get-tuple-element.34), channel_id=1, source_target_pairs={{1,0},{2,1},{3,2},{4,3},{5,4},{6,5},{7,6},{8,7},{9,8},{10,9},{11,1... | collective-permute-start | bytes 98312 | tf_op jit(solution)/shard_map/ppermute | solution.py:19
  244.7 1.0 copy-start.9
  246.2 18.0 %collective-permute-start.10 = (f32[1,64,128]{2,1,0:T(8,128)S(1)}, f32[1,64,128]{2,1,0:T(8,128)S(1)}, u32[]{:S(2)}, u32[]{:S(2)}) collective-permute-start(f32[1,64,128]{2,1,0:T(8,128)S(1)} %get-tuple-element.31), channel_id=1, source_target_pairs={{0,1},{1,2},{2,3},{3,4},{4,5},{5,6},{6,7},{7,8},{8,9},{9,10},{10,1... | collective-permute-start | bytes 98312 | tf_op jit(solution)/shard_map/ppermute | solution.py:16
  247.5 16.7 %collective-permute-start.11 = (f32[1,64,128]{2,1,0:T(8,128)S(1)}, f32[1,64,128]{2,1,0:T(8,128)S(1)}, u32[]{:S(2)}, u32[]{:S(2)}) collective-permute-start(f32[1,64,128]{2,1,0:T(8,128)S(1)} %get-tuple-element.32), channel_id=1, source_target_pairs={{1,0},{2,1},{3,2},{4,3},{5,4},{6,5},{7,6},{8,7},{9,8},{10,9},{11,1... | collective-permute-start | bytes 98312 | tf_op jit(solution)/shard_map/ppermute | solution.py:19
  248.9 16.2 %collective-permute-start.12 = (f32[12,16,128]{2,1,0:T(8,128)S(1)}, f32[12,16,128]{2,1,0:T(8,128)S(1)}, u32[]{:S(2)}, u32[]{:S(2)}) collective-permute-start(f32[12,16,128]{2,1,0:T(8,128)S(1)} %get-tuple-element.29), channel_id=1, source_target_pairs={{0,16},{16,32},{32,48},{48,64},{64,80},{80,96},{96,112},{112,128},... | collective-permute-start | bytes 294920 | tf_op jit(solution)/shard_map/ppermute | solution.py:27
  262.4 10.4 %collective-permute-start.13 = (f32[12,16,128]{2,1,0:T(8,128)S(1)}, f32[12,16,128]{2,1,0:T(8,128)S(1)}, u32[]{:S(2)}, u32[]{:S(2)}) collective-permute-start(f32[12,16,128]{2,1,0:T(8,128)S(1)} %get-tuple-element.30), channel_id=1, source_target_pairs={{16,0},{32,16},{48,32},{64,48},{80,64},{96,80},{112,96},{128,112},... | collective-permute-start | bytes 294920 | tf_op jit(solution)/shard_map/ppermute | solution.py:27
  369.6 0.6 copy-start.13
where the time goes:
time: 372 us; the launch traced here: 371 us
  blocking collectives  272 us (73%)
  starting transfers between devices  53.5 us (14%)
  matrix products  20.1 us (5%)
  waiting for transfers between devices  14.1 us (4%)
  local copies, waits for them, and re-layouts  6.39 us (2%)
  other arithmetic  4.42 us (1%)
    psum x2, blocking collectives, step_length(): lax.psum((jnp.sum(image * residual, axis=(0, 1)), jnp.sum(image * image,...  194 us
    all_gather x2, blocking collectives, coarse_direct(): lax.all_gather(projected, 'sub', axis=0, tiled=True)  77.6 us
    ppermute x4, starting transfers between devices, from_behind(): lax.ppermute(value, axis, [(source, source + steps) for source in range(i...  33.7 us
    dot_general x24, matrix products, tile_apply(): return jnp.einsum('bij,bjc->bic', tile_set, vector, precision=PRECISE)  16.5 us
    ppermute x4, waiting for transfers between devices, from_behind(): lax.ppermute(value, axis, [(source, source + steps) for source in range(i...  14 us
    ppermute x5, starting transfers between devices, extended(): lax.ppermute(lax.slice_in_dim(block, block.shape[dim] - width, None, axis...  13.3 us
  transfers between devices with their start and end apart: 14, of which 2 were waited for; matrix products, arithmetic and copies ran while one was open for 2% of the time, Pallas kernels for 0%

commit v1 on v0

--- a/solution.py
+++ b/solution.py
@@ -83,7 +83,12 @@
 
 def coarse_direct(basis_rows, inverse_rows, residual):
     projected = project(basis_rows, residual)
-    return fold_rows(inverse_rows, lax.all_gather(projected, "sub", axis=0, tiled=True))
+    return fold_rows(
+        inverse_rows,
+        jnp.concatenate(
+            lax.all_to_all(jnp.stack([projected] * lax.axis_size("sub")), "sub", 0, 0), axis=0
+        ),
+    )
 
 
 def operate(update, coupling, diagonal, sides):

time: 372 us -> 325 us (0.87)
  blocking collectives: 272 us -> 203 us
  waiting for transfers between devices: 14.1 us -> 23.8 us
  starting transfers between devices: 53.5 us -> 63 us
    all_gather x2 -> x0, blocking collectives: 77.6 us -> none  [coarse_direct(): lax.all_gather(projected, 'sub', axis=0, tiled=True)]
    all_to_all x0 -> x2, starting transfers between devices: none -> 17.4 us  [coarse_direct(): lax.all_to_all(jnp.stack([projected] * lax.axis_size('sub')), 'sub', 0, 0)]
    ppermute x4, starting transfers between devices: 33.7 us -> 23 us  [from_behind(): lax.ppermute(value, axis, [(source, source + steps) for source in range(i...]
    all_to_all x0 -> x2, waiting for transfers between devices: none -> 9.65 us  [coarse_direct(): lax.all_to_all(jnp.stack([projected] * lax.axis_size('sub')), 'sub', 0, 0)]
    psum x2, blocking collectives: 194 us -> 203 us  [step_length(): lax.psum((jnp.sum(image * residual, axis=(0, 1)), jnp.sum(image * image,...]
  transfers between devices with their start and end apart: 14 -> 16, of which waited for: 2 -> 4; matrix products, arithmetic and copies ran while one was open for 2% -> 7% of each run, Pallas kernels for 0% -> 0%
where the time goes in v1:
time: 325 us; the launch traced here: 324 us
  blocking collectives  203 us (62%)
  starting transfers between devices  63 us (19%)
  waiting for transfers between devices  23.8 us (7%)
  matrix products  23.7 us (7%)
  local copies, waits for them, and re-layouts  5.84 us (2%)
  other arithmetic  3.61 us (1%)
    psum x2, blocking collectives, step_length(): lax.psum((jnp.sum(image * residual, axis=(0, 1)), jnp.sum(image * image,...  203 us
    ppermute x4, starting transfers between devices, from_behind(): lax.ppermute(value, axis, [(source, source + steps) for source in range(i...  23 us
    dot_general x24, matrix products, tile_apply(): return jnp.einsum('bij,bjc->bic', tile_set, vector, precision=PRECISE)  18.1 us
    all_to_all x2, starting transfers between devices, coarse_direct(): lax.all_to_all(jnp.stack([projected] * lax.axis_size('sub')), 'sub', 0, 0)  17.4 us
    ppermute x5, starting transfers between devices, extended(): lax.ppermute(lax.slice_in_dim(block, block.shape[dim] - width, None, axis...  16.2 us
    ppermute x4, waiting for transfers between devices, from_behind(): lax.ppermute(value, axis, [(source, source + steps) for source in range(i...  14.1 us
    all_to_all x2, waiting for transfers between devices, coarse_direct(): lax.all_to_all(jnp.stack([projected] * lax.axis_size('sub')), 'sub', 0, 0)  9.65 us
  transfers between devices with their start and end apart: 16, of which 4 were waited for; matrix products, arithmetic and copies ran while one was open for 7% of the time, Pallas kernels for 0%

profile of v1, /device:TPU:1, one launch (start us, length us, event | category | flops | bytes accessed | tf_op | source)
XLA Modules:
  0.0 324.0 jit_solution(15447986709908389980)
XLA Ops:
  0.0 0.8 slice_bitcast_fusion.1
  0.8 3.9 %collective-permute-start.2 = (f32[1,64,128]{2,1,0:T(8,128)S(1)}, f32[1,64,128]{2,1,0:T(8,128)S(1)}, u32[]{:S(2)}, u32[]{:S(2)}) collective-permute-start(f32[1,64,128]{2,1,0:T(8,128)S(1)} %get-tuple-element.43), channel_id=1, source_target_pairs={{0,1},{1,2},{2,3},{3,4},{4,5},{5,6},{6,7},{7,8},{8,9},{9,10},{10,1... | collective-permute-start | bytes 98312 | tf_op jit(solution)/shard_map/ppermute | solution.py:16
  4.8 1.3 collective-permute-start.3
  6.1 0.9 pad_maximum_fusion.12
  7.0 4.0 %collective-permute-start = (f32[1,64,256]{2,1,0:T(8,128)S(1)}, f32[1,64,256]{2,1,0:T(8,128)S(1)}, u32[]{:S(2)}, u32[]{:S(2)}) collective-permute-start(f32[1,64,256]{2,1,0:T(8,128)S(1)} %get-tuple-element.13), channel_id=1, source_target_pairs={{0,1},{1,2},{2,3},{3,4},{4,5},{5,6},{6,7},{7,8},{8,9},{9,10},{10,1... | collective-permute-start | bytes 196616 | tf_op jit(solution)/shard_map/ppermute | solution.py:16
  11.0 1.3 collective-permute-start.1
  12.7 0.9 stack.4
  13.5 12.4 %all-to-all-start = ((f32[16,64,128]{2,1,0:T(8,128)}), f32[16,64,128]{2,1,0:T(8,128)}, u32[]{:S(2)}, u32[]{:S(2)}) async-start(f32[16,64,128]{2,1,0:T(8,128)} %stack.4), calls=%async_computation | async-start | bytes 1048576 | tf_op jit(solution)/shard_map/all_to_all | solution.py:89
  26.1 0.6 fusion.81
  26.9 0.9 fusion.28
  28.3 0.6 convolution_add_fusion.8
  29.1 0.9 fusion.24
  30.6 0.6 convolution_add_fusion.6
  31.3 0.9 fusion.20
  32.8 1.4 fusion.77
  34.3 4.5 %all-to-all-done = f32[16,64,128]{2,1,0:T(8,128)} async-done(((f32[16,64,128]{2,1,0:T(8,128)}), f32[16,64,128]{2,1,0:T(8,128)}, u32[]{:S(2)}, u32[]{:S(2)}) %all-to-all-start) | async-done | bytes 524320 | tf_op jit(solution)/shard_map/all_to_all | solution.py:89
  38.8 2.0 fusion.85
  41.3 0.9 copy.7
  42.2 1.2 fusion.53
  43.9 2.2 collective-permute-start.4
  46.1 1.3 collective-permute-start.5
  47.5 11.7 %collective-permute-start.6 = (f32[12,16,128]{2,1,0:T(8,128)S(1)}, f32[12,16,128]{2,1,0:T(8,128)S(1)}, u32[]{:S(2)}, u32[]{:S(2)}) collective-permute-start(f32[12,16,128]{2,1,0:T(8,128)S(1)} %get-tuple-element.39), channel_id=1, source_target_pairs={{0,16},{16,32},{32,48},{48,64},{64,80},{80,96},{96,112},{112,128},... | collective-permute-start | bytes 294920 | tf_op jit(solution)/shard_map/ppermute | solution.py:27
  59.2 2.1 collective-permute-start.7
  61.3 0.7 fusion.7
  62.1 7.0 %collective-permute-done.7 = f32[12,16,128]{2,1,0:T(8,128)S(1)} collective-permute-done((f32[12,16,128]{2,1,0:T(8,128)S(1)}, f32[12,16,128]{2,1,0:T(8,128)S(1)}, u32[]{:S(2)}, u32[]{:S(2)}) %collective-permute-start.7) | collective-permute-done | bytes 98336 | tf_op jit(solution)/shard_map/ppermute | solution.py:27
  69.4 101.0 %all-reduce.13 = (f32[128]{0:T(128)S(1)}, f32[128]{0:T(128)S(1)}) all-reduce(f32[128]{0:T(128)S(1)} %get-tuple-element.8, f32[128]{0:T(128)S(1)} %get-tuple-element.7), channel_id=1, replica_groups=mesh['sec'=32,'sub'=16] {'sec','sub'}, use_global_device_ids=true, to_apply=%region_1.0 | all-reduce | flops 256 | bytes 2048 | tf_op jit(solution)/shard_map/psum | solution.py:107
  170.5 3.7 %collective-permute-start.8 = (f32[1,64,128]{2,1,0:T(8,128)S(1)}, f32[1,64,128]{2,1,0:T(8,128)S(1)}, u32[]{:S(2)}, u32[]{:S(2)}) collective-permute-start(f32[1,64,128]{2,1,0:T(8,128)S(1)} %get-tuple-element.33), channel_id=1, source_target_pairs={{0,1},{1,2},{2,3},{3,4},{4,5},{5,6},{6,7},{7,8},{8,9},{9,10},{10,1... | collective-permute-start | bytes 98312 | tf_op jit(solution)/shard_map/ppermute | solution.py:16
  174.2 1.3 collective-permute-start.9
  175.9 0.9 stack.5
  176.8 5.0 %all-to-all-start.1 = ((f32[16,64,128]{2,1,0:T(8,128)}), f32[16,64,128]{2,1,0:T(8,128)}, u32[]{:S(2)}, u32[]{:S(2)}) async-start(f32[16,64,128]{2,1,0:T(8,128)} %stack.5), calls=%async_computation.1 | async-start | bytes 1048576 | tf_op jit(solution)/shard_map/all_to_all | solution.py:89
  181.9 0.6 fusion.75
  182.6 0.9 fusion.16
  184.1 0.6 convolution_add_fusion.3
  184.8 0.9 fusion.12
  186.4 0.6 convolution_add_fusion.1
  187.1 0.9 fusion.8
  188.6 1.4 fusion.71
  190.1 5.1 %all-to-all-done.1 = f32[16,64,128]{2,1,0:T(8,128)} async-done(((f32[16,64,128]{2,1,0:T(8,128)}), f32[16,64,128]{2,1,0:T(8,128)}, u32[]{:S(2)}, u32[]{:S(2)}) %all-to-all-start.1) | async-done | bytes 524320 | tf_op jit(solution)/shard_map/all_to_all | solution.py:89
  195.2 2.0 fusion.83
  197.9 0.8 copy-done.6
  199.3 2.3 collective-permute-start.10
  201.7 1.3 collective-permute-start.11
  203.0 7.3 %collective-permute-start.12 = (f32[12,16,128]{2,1,0:T(8,128)S(1)}, f32[12,16,128]{2,1,0:T(8,128)S(1)}, u32[]{:S(2)}, u32[]{:S(2)}) collective-permute-start(f32[12,16,128]{2,1,0:T(8,128)S(1)} %get-tuple-element.29), channel_id=1, source_target_pairs={{0,16},{16,32},{32,48},{48,64},{64,80},{80,96},{96,112},{112,128},... | collective-permute-start | bytes 294920 | tf_op jit(solution)/shard_map/ppermute | solution.py:27
  210.3 1.9 collective-permute-start.13
  212.2 0.7 fusion.6
  213.0 7.1 %collective-permute-done.13 = f32[12,16,128]{2,1,0:T(8,128)S(1)} collective-permute-done((f32[12,16,128]{2,1,0:T(8,128)S(1)}, f32[12,16,128]{2,1,0:T(8,128)S(1)}, u32[]{:S(2)}, u32[]{:S(2)}) %collective-permute-start.13) | collective-permute-done | bytes 98336 | tf_op jit(solution)/shard_map/ppermute | solution.py:27
  220.4 102.2 %all-reduce.12 = (f32[128]{0:T(128)S(1)}, f32[128]{0:T(128)S(1)}) all-reduce(f32[128]{0:T(128)S(1)} %get-tuple-element.6, f32[128]{0:T(128)S(1)} %get-tuple-element.5), channel_id=1, replica_groups=mesh['sec'=32,'sub'=16] {'sec','sub'}, use_global_device_ids=true, to_apply=%region_5.0 | all-reduce | flops 256 | bytes 2048 | tf_op jit(solution)/shard_map/psum | solution.py:107
  323.2 0.8 add_bitcast_fusion
  (77 shorter events, 8.4 us)
Async XLA Ops:
  0.0 38.8 %copy-start = (f32[1,64,1024]{2,1,0:T(8,128)S(1)}, f32[1,64,1024]{2,1,0:T(8,128)}, u32[]{:S(2)}) copy-start(f32[1,64,1024]{2,1,0:T(8,128)} %param.11) | copy-start | bytes 786436
  0.8 25.3 %collective-permute-start.2 = (f32[1,64,128]{2,1,0:T(8,128)S(1)}, f32[1,64,128]{2,1,0:T(8,128)S(1)}, u32[]{:S(2)}, u32[]{:S(2)}) collective-permute-start(f32[1,64,128]{2,1,0:T(8,128)S(1)} %get-tuple-element.43), channel_id=1, source_target_pairs={{0,1},{1,2},{2,3},{3,4},{4,5},{5,6},{6,7},{7,8},{8,9},{9,10},{10,1... | collective-permute-start | bytes 98312 | tf_op jit(solution)/shard_map/ppermute | solution.py:16
  4.8 21.3 %collective-permute-start.3 = (f32[1,64,128]{2,1,0:T(8,128)S(1)}, f32[1,64,128]{2,1,0:T(8,128)S(1)}, u32[]{:S(2)}, u32[]{:S(2)}) collective-permute-start(f32[1,64,128]{2,1,0:T(8,128)S(1)} %get-tuple-element.44), channel_id=1, source_target_pairs={{1,0},{2,1},{3,2},{4,3},{5,4},{6,5},{7,6},{8,7},{9,8},{10,9},{11,1... | collective-permute-start | bytes 98312 | tf_op jit(solution)/shard_map/ppermute | solution.py:19
  6.1 6.2 %copy-start.1 = (f32[1,12,64,128]{3,2,1,0:T(8,128)S(1)}, f32[1,12,64,128]{3,2,1,0:T(8,128)}, u32[]{:S(2)}) copy-start(f32[1,12,64,128]{3,2,1,0:T(8,128)} %param.6) | copy-start | bytes 1179652
  6.1 6.2 %copy-start.5 = (f32[1,64,768]{2,1,0:T(8,128)S(1)}, f32[1,64,768]{2,1,0:T(8,128)}, u32[]{:S(2)}) copy-start(f32[1,64,768]{2,1,0:T(8,128)} %param.10) | copy-start | bytes 589828
  7.0 19.0 %collective-permute-start = (f32[1,64,256]{2,1,0:T(8,128)S(1)}, f32[1,64,256]{2,1,0:T(8,128)S(1)}, u32[]{:S(2)}, u32[]{:S(2)}) collective-permute-start(f32[1,64,256]{2,1,0:T(8,128)S(1)} %get-tuple-element.13), channel_id=1, source_target_pairs={{0,1},{1,2},{2,3},{3,4},{4,5},{5,6},{6,7},{7,8},{8,9},{9,10},{10,1... | collective-permute-start | bytes 196616 | tf_op jit(solution)/shard_map/ppermute | solution.py:16
  11.0 15.0 %collective-permute-start.1 = (f32[1,64,256]{2,1,0:T(8,128)S(1)}, f32[1,64,256]{2,1,0:T(8,128)S(1)}, u32[]{:S(2)}, u32[]{:S(2)}) collective-permute-start(f32[1,64,256]{2,1,0:T(8,128)S(1)} %get-tuple-element.14), channel_id=1, source_target_pairs={{1,0},{2,1},{3,2},{4,3},{5,4},{6,5},{7,6},{8,7},{9,8},{10,9},{11,1... | collective-permute-start | bytes 196616 | tf_op jit(solution)/shard_map/ppermute | solution.py:19
  13.5 12.4 %copy-start.11 = (f32[1,12,32]{2,0,1:T(1,128)S(1)}, f32[1,12,32]{2,0,1:T(1,128)}, u32[]{:S(2)}) copy-start(f32[1,12,32]{2,0,1:T(1,128)} %param.9) | copy-start | bytes 4612
  13.5 12.5 %copy-start.2 = (f32[1,12,64,128]{3,2,1,0:T(8,128)S(1)}, f32[1,12,64,128]{3,2,1,0:T(8,128)}, u32[]{:S(2)}) copy-start(f32[1,12,64,128]{3,2,1,0:T(8,128)} %param.8) | copy-start | bytes 1179652
  13.5 12.5 %copy-start.3 = (f32[1,12,64,128]{3,2,1,0:T(8,128)S(1)}, f32[1,12,64,128]{3,2,1,0:T(8,128)}, u32[]{:S(2)}) copy-start(f32[1,12,64,128]{3,2,1,0:T(8,128)} %param.7) | copy-start | bytes 1179652
  13.5 25.3 %all-to-all-start = ((f32[16,64,128]{2,1,0:T(8,128)}), f32[16,64,128]{2,1,0:T(8,128)}, u32[]{:S(2)}, u32[]{:S(2)}) async-start(f32[16,64,128]{2,1,0:T(8,128)} %stack.4), calls=%async_computation | async-start | bytes 1048576 | tf_op jit(solution)/shard_map/all_to_all | solution.py:89
  43.9 17.4 %collective-permute-start.4 = (f32[1,64,128]{2,1,0:T(8,128)S(1)}, f32[1,64,128]{2,1,0:T(8,128)S(1)}, u32[]{:S(2)}, u32[]{:S(2)}) collective-permute-start(f32[1,64,128]{2,1,0:T(8,128)S(1)} %get-tuple-element.41), channel_id=1, source_target_pairs={{0,1},{1,2},{2,3},{3,4},{4,5},{5,6},{6,7},{7,8},{8,9},{9,10},{10,1... | collective-permute-start | bytes 98312 | tf_op jit(solution)/shard_map/ppermute | solution.py:16
  46.1 15.2 %collective-permute-start.5 = (f32[1,64,128]{2,1,0:T(8,128)S(1)}, f32[1,64,128]{2,1,0:T(8,128)S(1)}, u32[]{:S(2)}, u32[]{:S(2)}) collective-permute-start(f32[1,64,128]{2,1,0:T(8,128)S(1)} %get-tuple-element.42), channel_id=1, source_target_pairs={{1,0},{2,1},{3,2},{4,3},{5,4},{6,5},{7,6},{8,7},{9,8},{10,9},{11,1... | collective-permute-start | bytes 98312 | tf_op jit(solution)/shard_map/ppermute | solution.py:19
  47.5 14.6 %collective-permute-start.6 = (f32[12,16,128]{2,1,0:T(8,128)S(1)}, f32[12,16,128]{2,1,0:T(8,128)S(1)}, u32[]{:S(2)}, u32[]{:S(2)}) collective-permute-start(f32[12,16,128]{2,1,0:T(8,128)S(1)} %get-tuple-element.39), channel_id=1, source_target_pairs={{0,16},{16,32},{32,48},{48,64},{64,80},{80,96},{96,112},{112,128},... | collective-permute-start | bytes 294920 | tf_op jit(solution)/shard_map/ppermute | solution.py:27
  59.2 10.0 %collective-permute-start.7 = (f32[12,16,128]{2,1,0:T(8,128)S(1)}, f32[12,16,128]{2,1,0:T(8,128)S(1)}, u32[]{:S(2)}, u32[]{:S(2)}) collective-permute-start(f32[12,16,128]{2,1,0:T(8,128)S(1)} %get-tuple-element.40), channel_id=1, source_target_pairs={{16,0},{32,16},{48,32},{64,48},{80,64},{96,80},{112,96},{128,112},... | collective-permute-start | bytes 294920 | tf_op jit(solution)/shard_map/ppermute | solution.py:27
  170.5 5.1 %copy-start.12 = (f32[128]{0:T(128)}, f32[128]{0:T(128)S(1)}, u32[]{:S(2)}) copy-start(f32[128]{0:T(128)S(1)} %div.6) | copy-start | bytes 1540
  170.5 11.3 %collective-permute-start.8 = (f32[1,64,128]{2,1,0:T(8,128)S(1)}, f32[1,64,128]{2,1,0:T(8,128)S(1)}, u32[]{:S(2)}, u32[]{:S(2)}) collective-permute-start(f32[1,64,128]{2,1,0:T(8,128)S(1)} %get-tuple-element.33), channel_id=1, source_target_pairs={{0,1},{1,2},{2,3},{3,4},{4,5},{5,6},{6,7},{7,8},{8,9},{9,10},{10,1... | collective-permute-start | bytes 98312 | tf_op jit(solution)/shard_map/ppermute | solution.py:16
  174.2 7.6 %collective-permute-start.9 = (f32[1,64,128]{2,1,0:T(8,128)S(1)}, f32[1,64,128]{2,1,0:T(8,128)S(1)}, u32[]{:S(2)}, u32[]{:S(2)}) collective-permute-start(f32[1,64,128]{2,1,0:T(8,128)S(1)} %get-tuple-element.34), channel_id=1, source_target_pairs={{1,0},{2,1},{3,2},{4,3},{5,4},{6,5},{7,6},{8,7},{9,8},{10,9},{11,1... | collective-permute-start | bytes 98312 | tf_op jit(solution)/shard_map/ppermute | solution.py:19
  176.8 18.4 %all-to-all-start.1 = ((f32[16,64,128]{2,1,0:T(8,128)}), f32[16,64,128]{2,1,0:T(8,128)}, u32[]{:S(2)}, u32[]{:S(2)}) async-start(f32[16,64,128]{2,1,0:T(8,128)} %stack.5), calls=%async_computation.1 | async-start | bytes 1048576 | tf_op jit(solution)/shard_map/all_to_all | solution.py:89
  181.8 3.9 %copy-start.7 = (f32[1,64,128]{2,1,0:T(8,128)}, f32[1,64,128]{2,1,0:T(8,128)S(1)}, u32[]{:S(2)}) copy-start(f32[1,64,128]{2,1,0:T(8,128)S(1)} %collective-permute-done.8) | copy-start | bytes 98308
  181.9 3.9 %copy-start.9 = (f32[1,64,128]{2,1,0:T(8,128)}, f32[1,64,128]{2,1,0:T(8,128)S(1)}, u32[]{:S(2)}) copy-start(f32[1,64,128]{2,1,0:T(8,128)S(1)} %collective-permute-done.9) | copy-start | bytes 98308
  187.1 0.9 copy-start.8
  187.1 0.9 copy-start.10
  197.7 1.0 copy-start.6
  199.3 12.9 %copy-start.4 = (f32[1,12,64,128]{3,2,1,0:T(8,128)S(1)}, f32[1,12,64,128]{3,2,1,0:T(8,128)}, u32[]{:S(2)}) copy-start(f32[1,12,64,128]{3,2,1,0:T(8,128)} %param.7) | copy-start | bytes 1179652
  199.3 12.9 %collective-permute-start.10 = (f32[1,64,128]{2,1,0:T(8,128)S(1)}, f32[1,64,128]{2,1,0:T(8,128)S(1)}, u32[]{:S(2)}, u32[]{:S(2)}) collective-permute-start(f32[1,64,128]{2,1,0:T(8,128)S(1)} %get-tuple-element.31), channel_id=1, source_target_pairs={{0,1},{1,2},{2,3},{3,4},{4,5},{5,6},{6,7},{7,8},{8,9},{9,10},{10,1... | collective-permute-start | bytes 98312 | tf_op jit(solution)/shard_map/ppermute | solution.py:16
  201.7 10.5 %collective-permute-start.11 = (f32[1,64,128]{2,1,0:T(8,128)S(1)}, f32[1,64,128]{2,1,0:T(8,128)S(1)}, u32[]{:S(2)}, u32[]{:S(2)}) collective-permute-start(f32[1,64,128]{2,1,0:T(8,128)S(1)} %get-tuple-element.32), channel_id=1, source_target_pairs={{1,0},{2,1},{3,2},{4,3},{5,4},{6,5},{7,6},{8,7},{9,8},{10,9},{11,1... | collective-permute-start | bytes 98312 | tf_op jit(solution)/shard_map/ppermute | solution.py:19
  203.0 10.0 %collective-permute-start.12 = (f32[12,16,128]{2,1,0:T(8,128)S(1)}, f32[12,16,128]{2,1,0:T(8,128)S(1)}, u32[]{:S(2)}, u32[]{:S(2)}) collective-permute-start(f32[12,16,128]{2,1,0:T(8,128)S(1)} %get-tuple-element.29), channel_id=1, source_target_pairs={{0,16},{16,32},{32,48},{48,64},{64,80},{80,96},{96,112},{112,128},... | collective-permute-start | bytes 294920 | tf_op jit(solution)/shard_map/ppermute | solution.py:27
  210.3 9.8 %collective-permute-start.13 = (f32[12,16,128]{2,1,0:T(8,128)S(1)}, f32[12,16,128]{2,1,0:T(8,128)S(1)}, u32[]{:S(2)}, u32[]{:S(2)}) collective-permute-start(f32[12,16,128]{2,1,0:T(8,128)S(1)} %get-tuple-element.30), channel_id=1, source_target_pairs={{16,0},{32,16},{48,32},{64,48},{80,64},{96,80},{112,96},{128,112},... | collective-permute-start | bytes 294920 | tf_op jit(solution)/shard_map/ppermute | solution.py:27
  322.6 0.6 copy-start.13
